TPU v7x, 256 devices: a whole 4x4x8 slice. The times are simulated.
256 devices in a mesh: grp: 8 (over z), ep: 32 (over y, x, core).
Axes of the slice: x: 4, y: 4, z: 8, core: 2. Of those that a mesh axis runs over, the one named last changes fastest.
Arguments:
- pol_hidden: bfloat16 [10240, 1024], P(('grp', 'ep')), may hold values from -80 to 80
- ref_hidden: bfloat16 [10240, 1024], P(('grp', 'ep')), may hold values from -80 to 80
- pol_routes: int32 [10240, 8], P(('grp', 'ep')), may hold values from 0 to 63, all different within a row; in each aligned block of 40 rows (0 to 39, 40 to 79, ...) at most 7 rows name the same one
- ref_routes: int32 [10240, 8], P(('grp', 'ep')), may hold values from 0 to 63, all different within a row; in each aligned block of 40 rows (0 to 39, 40 to 79, ...) at most 7 rows name the same one
- pol_gates: float32 [10240, 8], P(('grp', 'ep')), may hold values from 0.02 to 0.3
- ref_gates: float32 [10240, 8], P(('grp', 'ep')), may hold values from 0.02 to 0.3
- w_gate: bfloat16 [64, 1024, 384], P('ep'), may hold values from -0.1875 to 0.1875
- w_up: bfloat16 [64, 1024, 384], P('ep'), may hold values from -0.1875 to 0.1875
- w_down: bfloat16 [64, 384, 1024], P('ep'), may hold values from -0.3125 to 0.3125
- norm_gain: float32 [1024], replicated, may hold values from 0.5 to 1.5
- vocab_head: bfloat16 [77824, 1024], P(('grp', 'ep')), may hold values from -2 to 2
- targets: int32 [10240], P(('grp', 'ep')), may hold values from 0 to 77823
- seq_lengths: int32 [256], replicated, may hold values from 1 to 1024, 10240 in all
- owners: int32 [256], replicated, may hold values from 0 to 255, each once
Outputs:
- token_ratio: float32 [10240], P(('grp', 'ep'))
- owned_mean: float32 [256], P(('grp', 'ep'))
Inputs may be any that keep to these rules, and one draw needn't show every extreme that they name: `pol_routes`: each row names 8 different experts; among the 40 rows of one device no expert is named by more than 7 rows, a bound that some block reaches. `ref_routes`: each row names 8 different experts; among the 40 rows of one device no expert is named by more than 7 rows, a bound that some block reaches. `seq_lengths`: the lengths sum to 10240; the longest is exactly 1024. `owners`: every device index appears exactly once.
All inputs are finite; a program needn't handle non-finite values.
Results may differ from a plain program's by a relative error of at most 0.0062.
Values may be sent and summed in bfloat16 or wider, within the bound.
A program may use at most 128 MiB of HBM per device.

v0:
```python
import jax
import jax.numpy as jnp
from jax import lax
from jax.sharding import PartitionSpec as P


def joined_2(value, axis, join):
    pieces = jax.tree.map(lambda part: lax.all_gather(part, axis), value)
    head = jax.tree.map(lambda part: part[0], pieces)
    tail = jax.tree.map(lambda part: part[1:], pieces)
    so_far, _ = lax.scan(lambda so_far, share: (join(so_far, share), None), head, tail)
    return so_far


def combine_stats(earlier_part, second):
    peak = jnp.maximum(earlier_part[0], second[0])
    totals = earlier_part[1] * jnp.exp(earlier_part[0] - peak) + second[1] * jnp.exp(
        second[0] - peak
    )
    return (peak, totals, earlier_part[2] + second[2])


def vocab_stats(row_block, weights, vocab_ids, wanted):
    logits = jnp.einsum("td,vd->tv", row_block, weights, preferred_element_type=jnp.float32)
    peak = jnp.max(logits, axis=1)
    totals = jnp.sum(jnp.exp(logits - peak[:, None]), axis=1)
    picked = jnp.sum(jnp.where(vocab_ids[None, :] == wanted[:, None], logits, 0.0), axis=1)
    return (peak, totals, picked)


def expert_tables(routes, gates, experts, capacity):
    route_hits = routes[:, :, None] == jnp.arange(experts, dtype=jnp.int32)[None, None, :]
    members = jnp.sum(route_hits.astype(jnp.int32), axis=1)
    earlier = jnp.cumsum(members, axis=0) - members
    placed = (members[:, :, None] > 0) & (
        earlier[:, :, None] == jnp.arange(capacity, dtype=jnp.int32)[None, None, :]
    )
    weight = jnp.sum(jnp.where(route_hits, gates[:, :, None], 0.0), axis=1)
    tok_count = routes.shape[0]
    picker = placed.astype(jnp.bfloat16).reshape(tok_count, experts * capacity)
    mixing = (weight[:, :, None] * placed.astype(jnp.float32)).reshape(
        tok_count, experts * capacity
    )
    return (picker, mixing)


def local(
    pol_hidden,
    ref_hidden,
    pol_routes,
    ref_routes,
    pol_gates,
    ref_gates,
    w_gate,
    w_up,
    w_down,
    norm_gain,
    vocab_head,
    targets,
    seq_lengths,
    owners,
):
    groups = lax.axis_size("ep")
    device_index = lax.axis_index(("grp", "ep"))
    local_experts = w_gate.shape[0]
    experts = local_experts * groups
    tok_count = pol_hidden.shape[0]
    width = pol_hidden.shape[1]
    fanout = pol_routes.shape[1]
    capacity = tok_count * fanout // experts + 2
    pol_pick, pol_mixing = expert_tables(pol_routes, pol_gates, experts, capacity)
    ref_pick, ref_mixing = expert_tables(ref_routes, ref_gates, experts, capacity)
    pol_send = jnp.einsum(
        "ts,td->sd", pol_pick, pol_hidden, preferred_element_type=jnp.float32
    ).astype(jnp.bfloat16)
    ref_send = jnp.einsum(
        "ts,td->sd", ref_pick, ref_hidden, preferred_element_type=jnp.float32
    ).astype(jnp.bfloat16)
    pol_send = pol_send.reshape(groups, local_experts, capacity, width)
    ref_send = ref_send.reshape(groups, local_experts, capacity, width)
    pol_part = lax.all_to_all(pol_send, "ep", split_axis=0, concat_axis=0, tiled=True)
    ref_part = lax.all_to_all(ref_send, "ep", split_axis=0, concat_axis=0, tiled=True)
    slots = pol_part.shape[2]
    joined = jnp.concatenate((pol_part, ref_part), axis=2)
    gate_act = jnp.einsum("nesd,edf->nesf", joined, w_gate, preferred_element_type=jnp.float32)
    up_act = jnp.einsum("nesd,edf->nesf", joined, w_up, preferred_element_type=jnp.float32)
    inner = (jax.nn.silu(gate_act) * up_act).astype(jnp.bfloat16)
    outputs = jnp.einsum(
        "nesf,efd->nesd", inner, w_down, preferred_element_type=jnp.float32
    ).astype(jnp.bfloat16)
    pol_back = lax.all_to_all(outputs[:, :, :slots], "ep", split_axis=0, concat_axis=0, tiled=True)
    ref_back = lax.all_to_all(outputs[:, :, slots:], "ep", split_axis=0, concat_axis=0, tiled=True)

    def mix_back(hidden, mixing, back):
        rows_back = back.reshape(experts * capacity, width).astype(jnp.float32)
        mixed = hidden.astype(jnp.float32) + jnp.dot(
            mixing, rows_back, precision=lax.Precision.HIGHEST
        )
        scale = lax.rsqrt(jnp.mean(mixed * mixed, axis=1, keepdims=True) + 1e-06)
        return (mixed * scale * norm_gain).astype(jnp.bfloat16)

    pol_normed = mix_back(pol_hidden, pol_mixing, pol_back)
    ref_normed = mix_back(ref_hidden, ref_mixing, ref_back)
    vocab_rows = vocab_head.shape[0]
    band = lax.axis_index("grp")
    pol_col, ref_col, wanted = (
        lax.all_gather(pol_normed, "grp", axis=0, tiled=True),
        lax.all_gather(ref_normed, "grp", axis=0, tiled=True),
        lax.all_gather(targets, "grp", axis=0, tiled=True),
    )
    col_count = wanted.shape[0]
    floor_value = jnp.full((2, col_count), -1e30, jnp.float32)
    blank = jnp.zeros((2, col_count), jnp.float32)
    piece = lax.all_gather(vocab_head, "ep", axis=0, tiled=True)
    count = piece.shape[0]
    place = jnp.arange(count, dtype=jnp.int32)
    vocab_ids = band * groups * vocab_rows + place
    pol_stats = vocab_stats(pol_col, piece, vocab_ids, wanted)
    ref_stats = vocab_stats(ref_col, piece, vocab_ids, wanted)
    fresh = tuple(
        (jnp.stack((pol_part, ref_part)) for pol_part, ref_part in zip(pol_stats, ref_stats))
    )
    stats = combine_stats((floor_value, blank, blank), fresh)
    peak, totals, picked = joined_2(stats, "grp", combine_stats)
    logprob = picked - (peak + jnp.log(totals))
    mine = lax.dynamic_slice_in_dim(logprob, band * tok_count, tok_count, axis=1)
    token_ratio = mine[0] - mine[1]
    offsets = jnp.cumsum(seq_lengths) - seq_lengths
    positions = device_index * tok_count + jnp.arange(tok_count, dtype=jnp.int32)
    inside = (positions[:, None] >= offsets[None, :]) & (
        positions[:, None] < (offsets + seq_lengths)[None, :]
    )
    partial_value = jnp.dot(
        token_ratio, inside.astype(jnp.float32), precision=lax.Precision.HIGHEST
    ) / seq_lengths.astype(jnp.float32)
    sums = lax.psum(partial_value, ("grp", "ep"))
    owned = jnp.sum(jnp.where(owners == device_index, sums, 0.0)).reshape(1)
    return (token_ratio, owned)


def solution(mesh):
    return jax.shard_map(
        local,
        mesh=mesh,
        in_specs=(
            P(("grp", "ep"), None),
            P(("grp", "ep"), None),
            P(("grp", "ep"), None),
            P(("grp", "ep"), None),
            P(("grp", "ep"), None),
            P(("grp", "ep"), None),
            P("ep", None, None),
            P("ep", None, None),
            P("ep", None, None),
            P(),
            P(("grp", "ep"), None),
            P(("grp", "ep")),
            P(),
            P(),
        ),
        out_specs=(P(("grp", "ep")), P(("grp", "ep"))),
        check_vma=False,
    )
```

profile of v0, /device:TPU:1, one launch (start us, length us, event | category | flops | bytes accessed | tf_op | source)
XLA Modules:
  0.0 389.7 jit_solution(15554492775969641314)
XLA Ops:
  7.9 0.8 copy.62
  11.8 2.0 copy.67
  13.7 8.7 %all-to-all-start = ((bf16[32,2,7,1024]{3,1,2,0:T(2,128)(2,1)}), bf16[32,2,7,1024]{3,1,2,0:T(2,128)(2,1)S(1)}, u32[]{:S(2)}, u32[]{:S(2)}) async-start(bf16[32,2,7,1024]{3,1,2,0:T(2,128)(2,1)} %copy.67), calls=%async_computation | async-start | bytes 1835008 | tf_op jit(solution)/shard_map/all_to_all | solution.py:81
  24.1 1.4 convolution_convert_fusion
  25.5 1.4 reshape.318
  27.0 2.0 copy.71
  28.9 12.9 %all-to-all-done = bf16[32,2,7,1024]{3,1,2,0:T(2,128)(2,1)S(1)} async-done(((bf16[32,2,7,1024]{3,1,2,0:T(2,128)(2,1)}), bf16[32,2,7,1024]{3,1,2,0:T(2,128)(2,1)S(1)}, u32[]{:S(2)}, u32[]{:S(2)}) %all-to-all-start) | async-done | bytes 917536 | tf_op jit(solution)/shard_map/all_to_all | solution.py:81
  41.8 0.9 copy-done.2
  42.7 5.4 %all-to-all-start.1 = ((bf16[32,2,7,1024]{3,1,2,0:T(2,128)(2,1)}), bf16[32,2,7,1024]{3,1,2,0:T(2,128)(2,1)}, u32[]{:S(2)}, u32[]{:S(2)}) async-start(bf16[32,2,7,1024]{3,1,2,0:T(2,128)(2,1)} %copy.71), calls=%async_computation.1 | async-start | bytes 1835008 | tf_op jit(solution)/shard_map/all_to_all | solution.py:82
  48.2 1.4 copy_dynamic-update-slice_fusion.1
  49.6 14.5 %all-to-all-done.1 = bf16[32,2,7,1024]{3,1,2,0:T(2,128)(2,1)} async-done(((bf16[32,2,7,1024]{3,1,2,0:T(2,128)(2,1)}), bf16[32,2,7,1024]{3,1,2,0:T(2,128)(2,1)}, u32[]{:S(2)}, u32[]{:S(2)}) %all-to-all-start.1) | async-done | bytes 917536 | tf_op jit(solution)/shard_map/all_to_all | solution.py:82
  64.1 1.5 copy_dynamic-update-slice_fusion
  65.8 2.2 fusion.9
  68.0 5.2 %convert_bitcast_fusion = bf16[32,2,14,1024]{3,0,2,1:T(8,128)(2,1)} fusion(bf16[2,384,1024]{2,1,0:T(8,128)(2,1)S(1)} %copy-done, bf16[32,2,14,1024]{3,0,2,1:T(8,128)(2,1)S(1)} %copy_dynamic-update-slice_fusion, bf16[2,1024,384]{2,1,0:T(8,128)(2,1)} %param.23, f32[32,2,14,384]{3,0,2,1:T(8,128)} %fusion.9), kind=kOutput, calls=%fused_computation.12 | convolution fusion | flops 1412268032 | bytes 8192000 | tf_op jit(solution)/shard_map/nesf,efd->nesd/dot_general | solution.py:88
  73.2 1.9 fusion.44
  75.2 1.9 copy.78
  77.1 3.9 all-to-all-start.3
  81.8 1.9 copy.74
  83.7 21.1 %all-to-all-done.3 = bf16[32,2,7,1024]{3,1,2,0:T(2,128)(2,1)S(1)} async-done(((bf16[32,2,7,1024]{3,1,2,0:T(2,128)(2,1)}), bf16[32,2,7,1024]{3,1,2,0:T(2,128)(2,1)S(1)}, u32[]{:S(2)}, u32[]{:S(2)}) %all-to-all-start.3) | async-done | bytes 917536 | tf_op jit(solution)/shard_map/all_to_all | solution.py:92
  104.8 6.1 %all-to-all-start.2 = ((bf16[32,2,7,1024]{3,1,2,0:T(2,128)(2,1)}), bf16[32,2,7,1024]{3,1,2,0:T(2,128)(2,1)S(1)}, u32[]{:S(2)}, u32[]{:S(2)}) async-start(bf16[32,2,7,1024]{3,1,2,0:T(2,128)(2,1)} %copy.74), calls=%async_computation.2 | async-start | bytes 1835008 | tf_op jit(solution)/shard_map/all_to_all | solution.py:91
  113.7 20.4 %all-reduce = s32[320]{0:T(512)S(1)} all-reduce(s32[320]{0:T(512)S(1)} %dynamic-update-slice), channel_id=1, replica_groups=mesh['grp'=8,'ep'=32] {'grp'}, use_global_device_ids=true, to_apply=%add | all-reduce | flops 320 | bytes 2560
  136.3 1.2 reshape.320
  139.4 1.7 multiply_reduce_fusion.1
  141.2 20.2 %all_gather.26 = bf16[320,1024]{1,0:T(8,128)(2,1)S(1)} all-gather(bf16[40,1024]{1,0:T(8,128)(2,1)S(1)} %get-tuple-element.71), channel_id=1, replica_groups=mesh['grp'=8,'ep'=32] {'grp'}, dimensions={0}, use_global_device_ids=true | all-gather | bytes 737280 | tf_op jit(solution)/shard_map/all_gather | solution.py:107
  161.4 20.5 %all_gather.28 = bf16[320,1024]{1,0:T(8,128)(2,1)S(1)} all-gather(bf16[40,1024]{1,0:T(8,128)(2,1)S(1)} %get-tuple-element.72), channel_id=1, replica_groups=mesh['grp'=8,'ep'=32] {'grp'}, dimensions={0}, use_global_device_ids=true | all-gather | bytes 737280 | tf_op jit(solution)/shard_map/all_gather | solution.py:108
  181.9 13.4 %fusion.45 = (f32[320]{0:T(512)S(1)}, f32[320,9728]{1,0:T(8,128)}) fusion(bf16[320,1024]{1,0:T(8,128)(2,1)S(1)} %all_gather.26, bf16[9728,1024]{1,0:T(8,128)(2,1)} %all-gather.4.cloned.1.call-done), kind=kOutput, calls=%fused_computation.84 | convolution fusion | flops 6378454528 | bytes 33031424 | tf_op jit(solution)/shard_map/td,vd->tv/dot_general | solution.py:24
  195.3 13.5 %fusion.46 = (f32[320]{0:T(512)S(1)}, f32[320,9728]{1,0:T(8,128)}) fusion(bf16[320,1024]{1,0:T(8,128)(2,1)S(1)} %all_gather.28, bf16[9728,1024]{1,0:T(8,128)(2,1)} %all-gather.4.cloned.1.call-done), kind=kOutput, calls=%fused_computation.85 | convolution fusion | flops 6378454528 | bytes 33031424 | tf_op jit(solution)/shard_map/td,vd->tv/dot_general | solution.py:24
  208.8 11.5 %fusion.2 = (f32[320]{0:T(512)S(1)}, f32[320]{0:T(512)S(1)}, f32[320]{0:T(512)S(1)}, f32[320]{0:T(512)S(1)}) fusion(f32[320,9728]{1,0:T(8,128)} %get-tuple-element.80, s32[9728]{0:T(1024)S(1)} %copy-done.17, s32[320]{0:T(512)S(1)} %all-reduce, f32[320]{0:T(512)S(1)} %get-tuple-element.79, f32[320,9728]{1,0:T(8,128)} %get-tuple-element.82, ...), kind=kLoop, calls=%fused_computation.8 | loop fusion | flops 28015360 | bytes 24951552 | tf_op jit(solution)/shard_map/reduce_sum | solution.py:27
  220.3 18.0 %all-gather.1 = f32[8,2,320]{2,1,0:T(2,128)S(1)} all-gather(f32[1,2,320]{2,1,0:T(2,128)S(1)} %maximum_bitcast_fusion), channel_id=2, replica_groups=mesh['grp'=8,'ep'=32] {'grp'}, dimensions={0}, use_global_device_ids=true | all-gather | bytes 23040 | tf_op jit(solution)/shard_map/all_gather | solution.py:8
  238.4 18.0 %all_gather.30 = f32[8,2,320]{2,1,0:T(2,128)S(1)} all-gather(f32[1,2,320]{2,1,0:T(2,128)S(1)} %get-tuple-element.73), channel_id=1, replica_groups=mesh['grp'=8,'ep'=32] {'grp'}, dimensions={0}, use_global_device_ids=true | all-gather | bytes 23040 | tf_op jit(solution)/shard_map/all_gather | solution.py:8
  256.5 18.0 %all_gather.29 = f32[8,2,320]{2,1,0:T(2,128)S(1)} all-gather(f32[1,2,320]{2,1,0:T(2,128)S(1)} %get-tuple-element.74), channel_id=1, replica_groups=mesh['grp'=8,'ep'=32] {'grp'}, dimensions={0}, use_global_device_ids=true | all-gather | bytes 23040 | tf_op jit(solution)/shard_map/all_gather | solution.py:8
  275.7 106.6 %psum.7 = f32[256]{0:T(256)S(1)} all-reduce(f32[256]{0:T(256)S(1)} %convert_divide_fusion), channel_id=1, replica_groups=mesh['grp'=8,'ep'=32] {'grp','ep'}, use_global_device_ids=true, to_apply=%region_18.19 | all-reduce | flops 256 | bytes 2048 | tf_op jit(solution)/shard_map/psum | solution.py:136
  (141 shorter events, 14.5 us)
Async XLA Ops:
  7.2 60.8 %copy-start = (bf16[2,384,1024]{2,1,0:T(8,128)(2,1)S(1)}, bf16[2,384,1024]{2,1,0:T(8,128)(2,1)}, u32[]{:S(2)}) copy-start(bf16[2,384,1024]{2,1,0:T(8,128)(2,1)} %param.24) | copy-start | bytes 4718596
  7.2 3.8 copy-start.7
  7.2 174.7 %all-gather.4.cloned.1.call-start = ((), (), s32[]{:S(2)}) async-start(), calls=%async_computation.4 | async-start | bytes 20545536 | tf_op jit(solution)/shard_map/all_gather | solution.py:114
  9.4 0.6 copy-start.9
  11.7 10.7 %copy-start.22 = (s32[40,8]{0,1:T(8,128)S(1)}, s32[40,8]{0,1:T(8,128)}, u32[]{:S(2)}) copy-start(s32[40,8]{0,1:T(8,128)} %param.19) | copy-start | bytes 3844
  13.7 10.4 %copy-start.5 = (bf16[40,1024]{1,0:T(8,128)(2,1)S(1)}, bf16[40,1024]{1,0:T(8,128)(2,1)}, u32[]{:S(2)}) copy-start(bf16[40,1024]{1,0:T(8,128)(2,1)} %param.17) | copy-start | bytes 245764
  13.7 10.4 %copy-start.19 = (s32[448]{0:T(512)S(1)}, s32[448]{0:T(512)}, u32[]{:S(2)}) copy-start(s32[448]{0:T(512)} %copy-done.18) | copy-start | bytes 5380
  13.7 28.1 %all-to-all-start = ((bf16[32,2,7,1024]{3,1,2,0:T(2,128)(2,1)}), bf16[32,2,7,1024]{3,1,2,0:T(2,128)(2,1)S(1)}, u32[]{:S(2)}, u32[]{:S(2)}) async-start(bf16[32,2,7,1024]{3,1,2,0:T(2,128)(2,1)} %copy.67), calls=%async_computation | async-start | bytes 1835008 | tf_op jit(solution)/shard_map/all_to_all | solution.py:81
  23.2 0.6 copy-start.11
  41.8 0.9 copy-start.2
  42.7 21.4 %all-to-all-start.1 = ((bf16[32,2,7,1024]{3,1,2,0:T(2,128)(2,1)}), bf16[32,2,7,1024]{3,1,2,0:T(2,128)(2,1)}, u32[]{:S(2)}, u32[]{:S(2)}) async-start(bf16[32,2,7,1024]{3,1,2,0:T(2,128)(2,1)} %copy.71), calls=%async_computation.1 | async-start | bytes 1835008 | tf_op jit(solution)/shard_map/all_to_all | solution.py:82
  64.1 1.7 copy-start.4
  75.2 5.8 %copy-start.23 = (f32[40,8]{0,1:T(8,128)S(1)}, f32[40,8]{0,1:T(8,128)}, u32[]{:S(2)}) copy-start(f32[40,8]{0,1:T(8,128)} %param.21) | copy-start | bytes 3844
  75.2 5.9 %copy-start.16 = (s32[40,8]{1,0:T(8,128)S(1)}, s32[40,8]{1,0:T(8,128)}, u32[]{:S(2)}) copy-start(s32[40,8]{1,0:T(8,128)} %copy-done.15) | copy-start | bytes 3844
  75.2 6.1 %copy-start.12 = (s32[40,64]{0,1:T(8,128)S(1)}, s32[40,64]{0,1:T(8,128)}, u32[]{:S(2)}) copy-start(s32[40,64]{0,1:T(8,128)} %copy-done.11) | copy-start | bytes 30724
  77.1 4.4 %copy-start.24 = (f32[40,8]{0,1:T(8,128)S(1)}, f32[40,8]{0,1:T(8,128)}, u32[]{:S(2)}) copy-start(f32[40,8]{0,1:T(8,128)} %param.20) | copy-start | bytes 3844
  77.1 4.4 %copy-start.14 = (s32[40,8]{1,0:T(8,128)S(1)}, s32[40,8]{1,0:T(8,128)}, u32[]{:S(2)}) copy-start(s32[40,8]{1,0:T(8,128)} %copy-done.13) | copy-start | bytes 3844
  77.1 27.7 %all-to-all-start.3 = ((bf16[32,2,7,1024]{3,1,2,0:T(2,128)(2,1)}), bf16[32,2,7,1024]{3,1,2,0:T(2,128)(2,1)S(1)}, u32[]{:S(2)}, u32[]{:S(2)}) async-start(bf16[32,2,7,1024]{3,1,2,0:T(2,128)(2,1)} %copy.78), calls=%async_computation.3 | async-start | bytes 1835008 | tf_op jit(solution)/shard_map/all_to_all | solution.py:92
  81.8 29.2 %copy-start.10 = (s32[40,64]{0,1:T(8,128)S(1)}, s32[40,64]{0,1:T(8,128)}, u32[]{:S(2)}) copy-start(s32[40,64]{0,1:T(8,128)} %copy-done.9) | copy-start | bytes 30724
  81.8 30.0 %copy-start.20 = (s32[256]{0:T(256)S(1)}, s32[256]{0:T(256)}, u32[]{:S(2)}) copy-start(s32[256]{0:T(256)} %param.28) | copy-start | bytes 3076
  81.8 30.4 %copy-start.28 = (u32[256]{0:T(256)S(1)}, u32[256]{0:T(256)}, u32[]{:S(2)}) copy-start(u32[256]{0:T(256)} %constant.68) | copy-start | bytes 3076
  81.8 31.6 %copy-start.27 = (s32[40]{0:T(128)S(1)}, s32[40]{0:T(128)}, u32[]{:S(2)}) copy-start(s32[40]{0:T(128)} %param.27) | copy-start | bytes 484
  104.8 32.7 %all-to-all-start.2 = ((bf16[32,2,7,1024]{3,1,2,0:T(2,128)(2,1)}), bf16[32,2,7,1024]{3,1,2,0:T(2,128)(2,1)S(1)}, u32[]{:S(2)}, u32[]{:S(2)}) async-start(bf16[32,2,7,1024]{3,1,2,0:T(2,128)(2,1)} %copy.74), calls=%async_computation.2 | async-start | bytes 1835008 | tf_op jit(solution)/shard_map/all_to_all | solution.py:91
  137.5 1.2 copy-start.3
  137.5 1.2 copy-start.6
  137.8 1.6 copy-start.8
  138.7 2.4 copy-start.21
  195.3 13.5 %copy-start.17 = (s32[9728]{0:T(1024)S(1)}, s32[9728]{0:T(1024)}, u32[]{:S(2)}) copy-start(s32[9728]{0:T(1024)} %iota_add_fusion) | copy-start | bytes 116740
  208.8 66.7 %copy-start.26 = (s32[256]{0:T(256)S(1)}, s32[256]{0:T(256)}, u32[]{:S(2)}) copy-start(s32[256]{0:T(256)} %get-tuple-element.67) | copy-start | bytes 3076
  208.8 66.7 %copy-start.29 = (s32[40]{0:T(128)S(1)}, s32[40]{0:T(128)}, u32[]{:S(2)}) copy-start(s32[40]{0:T(128)} %iota_add_fusion.1) | copy-start | bytes 484
  208.8 173.4 %copy-start.25 = (s32[256]{0:T(256)S(1)}, s32[256]{0:T(256)}, u32[]{:S(2)}) copy-start(s32[256]{0:T(256)} %param.29) | copy-start | bytes 3076
  208.8 174.0 %copy-start.1 = (bf16[2,384,1024]{2,1,0:T(8,128)(2,1)S(1)}, bf16[2,384,1024]{2,1,0:T(8,128)(2,1)}, u32[]{:S(2)}) copy-start(bf16[2,384,1024]{2,1,0:T(8,128)(2,1)} %param.24) | copy-start | bytes 4718596
  (3 other events, 1.8 us)
Sparse Core Ops, SparseCore 0:
  10.6 105.0 all-gather.3
where the time goes:
time: 391 us; the launch traced here: 390 us
  blocking collectives  222 us (57%)
  waiting for transfers between devices  49.2 us (13%)
  matrix products  38.7 us (10%)
  local copies, waits for them, and re-layouts  24.4 us (6%)
  starting transfers between devices  24.2 us (6%)
  other arithmetic  16.1 us (4%)
  between operations  15.3 us (4%)
    psum x1, blocking collectives, local(): sums = lax.psum(partial_value, ('grp', 'ep'))  107 us
    all_gather x3, blocking collectives, joined_2(): pieces = jax.tree.map(lambda part: lax.all_gather(part, axis), value)  54 us
    dot_general x2, matrix products, vocab_stats(): jnp.einsum('td,vd->tv', row_block, weights, preferred_element_type=jnp.fl...  26.9 us
    all_to_all x1, waiting for transfers between devices, local(): lax.all_to_all(outputs[:, :, slots:], 'ep', split_axis=0, concat_axis=0,...  21.1 us
    all_gather x1, blocking collectives, local(): lax.all_gather(ref_normed, 'grp', axis=0, tiled=True)  20.5 us
    unnamed x1, blocking collectives  20.4 us
    all_gather x1, blocking collectives, local(): lax.all_gather(pol_normed, 'grp', axis=0, tiled=True)  20.2 us
    all_to_all x1, waiting for transfers between devices, local(): lax.all_to_all(ref_send, 'ep', split_axis=0, concat_axis=0, tiled=True)  14.5 us
  transfers between devices with their start and end apart: 5, of which 3 were waited for; matrix products, arithmetic and copies ran while one was open for 9% of the time, Pallas kernels for 0%

commit v1 on v0

--- a/solution.py
+++ b/solution.py
@@ -133,7 +133,8 @@
     partial_value = jnp.dot(
         token_ratio, inside.astype(jnp.float32), precision=lax.Precision.HIGHEST
     ) / seq_lengths.astype(jnp.float32)
-    sums = lax.psum(partial_value, ("grp", "ep"))
+    parts = lax.all_gather(partial_value, ("grp", "ep"))
+    sums = jnp.sum(parts, axis=0)
     owned = jnp.sum(jnp.where(owners == device_index, sums, 0.0)).reshape(1)
     return (token_ratio, owned)
 

time: 391 us -> 379 us (0.969)
  blocking collectives: 222 us -> 210 us
    psum x1 -> x0, blocking collectives: 107 us -> none  [local(): sums = lax.psum(partial_value, ('grp', 'ep'))]
    all_gather x0 -> x1, blocking collectives: none -> 94.4 us  [local(): parts = lax.all_gather(partial_value, ('grp', 'ep'))]
where the time goes in v1:
time: 379 us; the launch traced here: 378 us
  blocking collectives  210 us (55%)
  waiting for transfers between devices  49.2 us (13%)
  matrix products  38.7 us (10%)
  local copies, waits for them, and re-layouts  24.4 us (6%)
  starting transfers between devices  24.2 us (6%)
  other arithmetic  16.4 us (4%)
  between operations  15.3 us (4%)
    all_gather x1, blocking collectives, local(): parts = lax.all_gather(partial_value, ('grp', 'ep'))  94.4 us
    all_gather x3, blocking collectives, joined_2(): pieces = jax.tree.map(lambda part: lax.all_gather(part, axis), value)  54 us
    dot_general x2, matrix products, vocab_stats(): jnp.einsum('td,vd->tv', row_block, weights, preferred_element_type=jnp.fl...  26.9 us
    all_to_all x1, waiting for transfers between devices, local(): lax.all_to_all(outputs[:, :, slots:], 'ep', split_axis=0, concat_axis=0,...  21.1 us
    all_gather x1, blocking collectives, local(): lax.all_gather(ref_normed, 'grp', axis=0, tiled=True)  20.5 us
    unnamed x1, blocking collectives  20.4 us
    all_gather x1, blocking collectives, local(): lax.all_gather(pol_normed, 'grp', axis=0, tiled=True)  20.2 us
    all_to_all x1, waiting for transfers between devices, local(): lax.all_to_all(ref_send, 'ep', split_axis=0, concat_axis=0, tiled=True)  14.5 us
  transfers between devices with their start and end apart: 5, of which 3 were waited for; matrix products, arithmetic and copies ran while one was open for 9% of the time, Pallas kernels for 0%

profile of v1, /device:TPU:1, one launch (start us, length us, event | category | flops | bytes accessed | tf_op | source)
XLA Modules:
  0.0 377.9 jit_solution(11157705221089676749)
XLA Ops:
  7.9 0.8 copy.62
  11.8 2.0 copy.67
  13.7 8.7 %all-to-all-start = ((bf16[32,2,7,1024]{3,1,2,0:T(2,128)(2,1)}), bf16[32,2,7,1024]{3,1,2,0:T(2,128)(2,1)S(1)}, u32[]{:S(2)}, u32[]{:S(2)}) async-start(bf16[32,2,7,1024]{3,1,2,0:T(2,128)(2,1)} %copy.67), calls=%async_computation | async-start | bytes 1835008 | tf_op jit(solution)/shard_map/all_to_all | solution.py:81
  24.1 1.4 convolution_convert_fusion
  25.5 1.4 reshape.318
  27.0 2.0 copy.71
  28.9 12.9 %all-to-all-done = bf16[32,2,7,1024]{3,1,2,0:T(2,128)(2,1)S(1)} async-done(((bf16[32,2,7,1024]{3,1,2,0:T(2,128)(2,1)}), bf16[32,2,7,1024]{3,1,2,0:T(2,128)(2,1)S(1)}, u32[]{:S(2)}, u32[]{:S(2)}) %all-to-all-start) | async-done | bytes 917536 | tf_op jit(solution)/shard_map/all_to_all | solution.py:81
  41.8 0.9 copy-done.2
  42.7 5.4 %all-to-all-start.1 = ((bf16[32,2,7,1024]{3,1,2,0:T(2,128)(2,1)}), bf16[32,2,7,1024]{3,1,2,0:T(2,128)(2,1)}, u32[]{:S(2)}, u32[]{:S(2)}) async-start(bf16[32,2,7,1024]{3,1,2,0:T(2,128)(2,1)} %copy.71), calls=%async_computation.1 | async-start | bytes 1835008 | tf_op jit(solution)/shard_map/all_to_all | solution.py:82
  48.2 1.4 copy_dynamic-update-slice_fusion.1
  49.6 14.5 %all-to-all-done.1 = bf16[32,2,7,1024]{3,1,2,0:T(2,128)(2,1)} async-done(((bf16[32,2,7,1024]{3,1,2,0:T(2,128)(2,1)}), bf16[32,2,7,1024]{3,1,2,0:T(2,128)(2,1)}, u32[]{:S(2)}, u32[]{:S(2)}) %all-to-all-start.1) | async-done | bytes 917536 | tf_op jit(solution)/shard_map/all_to_all | solution.py:82
  64.1 1.5 copy_dynamic-update-slice_fusion
  65.8 2.2 fusion.9
  68.0 5.2 %convert_bitcast_fusion = bf16[32,2,14,1024]{3,0,2,1:T(8,128)(2,1)} fusion(bf16[2,384,1024]{2,1,0:T(8,128)(2,1)S(1)} %copy-done, bf16[32,2,14,1024]{3,0,2,1:T(8,128)(2,1)S(1)} %copy_dynamic-update-slice_fusion, bf16[2,1024,384]{2,1,0:T(8,128)(2,1)} %param.23, f32[32,2,14,384]{3,0,2,1:T(8,128)} %fusion.9), kind=kOutput, calls=%fused_computation.12 | convolution fusion | flops 1412268032 | bytes 8192000 | tf_op jit(solution)/shard_map/nesf,efd->nesd/dot_general | solution.py:88
  73.2 1.9 fusion.44
  75.2 1.9 copy.78
  77.1 3.9 %all-to-all-start.3 = ((bf16[32,2,7,1024]{3,1,2,0:T(2,128)(2,1)}), bf16[32,2,7,1024]{3,1,2,0:T(2,128)(2,1)S(1)}, u32[]{:S(2)}, u32[]{:S(2)}) async-start(bf16[32,2,7,1024]{3,1,2,0:T(2,128)(2,1)} %copy.78), calls=%async_computation.3 | async-start | bytes 1835008 | tf_op jit(solution)/shard_map/all_to_all | solution.py:92
  81.8 1.9 copy.74
  83.7 21.1 %all-to-all-done.3 = bf16[32,2,7,1024]{3,1,2,0:T(2,128)(2,1)S(1)} async-done(((bf16[32,2,7,1024]{3,1,2,0:T(2,128)(2,1)}), bf16[32,2,7,1024]{3,1,2,0:T(2,128)(2,1)S(1)}, u32[]{:S(2)}, u32[]{:S(2)}) %all-to-all-start.3) | async-done | bytes 917536 | tf_op jit(solution)/shard_map/all_to_all | solution.py:92
  104.8 6.1 %all-to-all-start.2 = ((bf16[32,2,7,1024]{3,1,2,0:T(2,128)(2,1)}), bf16[32,2,7,1024]{3,1,2,0:T(2,128)(2,1)S(1)}, u32[]{:S(2)}, u32[]{:S(2)}) async-start(bf16[32,2,7,1024]{3,1,2,0:T(2,128)(2,1)} %copy.74), calls=%async_computation.2 | async-start | bytes 1835008 | tf_op jit(solution)/shard_map/all_to_all | solution.py:91
  113.7 20.4 %all-reduce = s32[320]{0:T(512)S(1)} all-reduce(s32[320]{0:T(512)S(1)} %dynamic-update-slice), channel_id=1, replica_groups=mesh['grp'=8,'ep'=32] {'grp'}, use_global_device_ids=true, to_apply=%add | all-reduce | flops 320 | bytes 2560
  136.3 1.2 reshape.320
  139.4 1.7 multiply_reduce_fusion.1
  141.2 20.2 %all_gather.32 = bf16[320,1024]{1,0:T(8,128)(2,1)S(1)} all-gather(bf16[40,1024]{1,0:T(8,128)(2,1)S(1)} %get-tuple-element.71), channel_id=1, replica_groups=mesh['grp'=8,'ep'=32] {'grp'}, dimensions={0}, use_global_device_ids=true | all-gather | bytes 737280 | tf_op jit(solution)/shard_map/all_gather | solution.py:107
  161.4 20.5 %all_gather.34 = bf16[320,1024]{1,0:T(8,128)(2,1)S(1)} all-gather(bf16[40,1024]{1,0:T(8,128)(2,1)S(1)} %get-tuple-element.72), channel_id=1, replica_groups=mesh['grp'=8,'ep'=32] {'grp'}, dimensions={0}, use_global_device_ids=true | all-gather | bytes 737280 | tf_op jit(solution)/shard_map/all_gather | solution.py:108
  181.9 13.4 %fusion.45 = (f32[320]{0:T(512)S(1)}, f32[320,9728]{1,0:T(8,128)}) fusion(bf16[320,1024]{1,0:T(8,128)(2,1)S(1)} %all_gather.32, bf16[9728,1024]{1,0:T(8,128)(2,1)} %all-gather.6.cloned.1.call-done), kind=kOutput, calls=%fused_computation.84 | convolution fusion | flops 6378454528 | bytes 33031424 | tf_op jit(solution)/shard_map/td,vd->tv/dot_general | solution.py:24
  195.3 13.5 %fusion.46 = (f32[320]{0:T(512)S(1)}, f32[320,9728]{1,0:T(8,128)}) fusion(bf16[320,1024]{1,0:T(8,128)(2,1)S(1)} %all_gather.34, bf16[9728,1024]{1,0:T(8,128)(2,1)} %all-gather.6.cloned.1.call-done), kind=kOutput, calls=%fused_computation.85 | convolution fusion | flops 6378454528 | bytes 33031424 | tf_op jit(solution)/shard_map/td,vd->tv/dot_general | solution.py:24
  208.8 11.5 %fusion.2 = (f32[320]{0:T(512)S(1)}, f32[320]{0:T(512)S(1)}, f32[320]{0:T(512)S(1)}, f32[320]{0:T(512)S(1)}) fusion(f32[320,9728]{1,0:T(8,128)} %get-tuple-element.80, s32[9728]{0:T(1024)S(1)} %copy-done.17, s32[320]{0:T(512)S(1)} %all-reduce, f32[320]{0:T(512)S(1)} %get-tuple-element.79, f32[320,9728]{1,0:T(8,128)} %get-tuple-element.82, ...), kind=kLoop, calls=%fused_computation.8 | loop fusion | flops 28015360 | bytes 24951552 | tf_op jit(solution)/shard_map/reduce_sum | solution.py:27
  220.3 18.0 %all-gather.2 = f32[8,2,320]{2,1,0:T(2,128)S(1)} all-gather(f32[1,2,320]{2,1,0:T(2,128)S(1)} %maximum_bitcast_fusion), channel_id=2, replica_groups=mesh['grp'=8,'ep'=32] {'grp'}, dimensions={0}, use_global_device_ids=true | all-gather | bytes 23040 | tf_op jit(solution)/shard_map/all_gather | solution.py:8
  238.4 18.0 %all_gather.36 = f32[8,2,320]{2,1,0:T(2,128)S(1)} all-gather(f32[1,2,320]{2,1,0:T(2,128)S(1)} %get-tuple-element.73), channel_id=1, replica_groups=mesh['grp'=8,'ep'=32] {'grp'}, dimensions={0}, use_global_device_ids=true | all-gather | bytes 23040 | tf_op jit(solution)/shard_map/all_gather | solution.py:8
  256.5 18.0 %all_gather.35 = f32[8,2,320]{2,1,0:T(2,128)S(1)} all-gather(f32[1,2,320]{2,1,0:T(2,128)S(1)} %get-tuple-element.74), channel_id=1, replica_groups=mesh['grp'=8,'ep'=32] {'grp'}, dimensions={0}, use_global_device_ids=true | all-gather | bytes 23040 | tf_op jit(solution)/shard_map/all_gather | solution.py:8
  275.7 94.4 %all-gather.3 = f32[256,1,256]{2,1,0:T(1,128)S(1)} all-gather(f32[1,1,256]{2,1,0:T(1,128)S(1)} %bitcast.99), channel_id=3, replica_groups=mesh['grp'=8,'ep'=32] {'grp','ep'}, dimensions={0}, use_global_device_ids=true | all-gather | bytes 263168 | tf_op jit(solution)/shard_map/all_gather | solution.py:136
  (142 shorter events, 14.8 us)
Async XLA Ops:
  7.2 60.8 %copy-start = (bf16[2,384,1024]{2,1,0:T(8,128)(2,1)S(1)}, bf16[2,384,1024]{2,1,0:T(8,128)(2,1)}, u32[]{:S(2)}) copy-start(bf16[2,384,1024]{2,1,0:T(8,128)(2,1)} %param.24) | copy-start | bytes 4718596
  7.2 3.8 %copy-start.7 = (bf16[40,1024]{1,0:T(8,128)(2,1)S(1)}, bf16[40,1024]{1,0:T(8,128)(2,1)}, u32[]{:S(2)}) copy-start(bf16[40,1024]{1,0:T(8,128)(2,1)} %param.16) | copy-start | bytes 245764
  7.2 174.7 %all-gather.6.cloned.1.call-start = ((), (), s32[]{:S(2)}) async-start(), calls=%async_computation.4 | async-start | bytes 20545536 | tf_op jit(solution)/shard_map/all_gather | solution.py:114
  9.4 0.6 copy-start.9
  11.7 10.7 %copy-start.22 = (s32[40,8]{0,1:T(8,128)S(1)}, s32[40,8]{0,1:T(8,128)}, u32[]{:S(2)}) copy-start(s32[40,8]{0,1:T(8,128)} %param.19) | copy-start | bytes 3844
  13.7 10.4 %copy-start.5 = (bf16[40,1024]{1,0:T(8,128)(2,1)S(1)}, bf16[40,1024]{1,0:T(8,128)(2,1)}, u32[]{:S(2)}) copy-start(bf16[40,1024]{1,0:T(8,128)(2,1)} %param.17) | copy-start | bytes 245764
  13.7 10.4 %copy-start.19 = (s32[448]{0:T(512)S(1)}, s32[448]{0:T(512)}, u32[]{:S(2)}) copy-start(s32[448]{0:T(512)} %copy-done.18) | copy-start | bytes 5380
  13.7 28.1 %all-to-all-start = ((bf16[32,2,7,1024]{3,1,2,0:T(2,128)(2,1)}), bf16[32,2,7,1024]{3,1,2,0:T(2,128)(2,1)S(1)}, u32[]{:S(2)}, u32[]{:S(2)}) async-start(bf16[32,2,7,1024]{3,1,2,0:T(2,128)(2,1)} %copy.67), calls=%async_computation | async-start | bytes 1835008 | tf_op jit(solution)/shard_map/all_to_all | solution.py:81
  23.2 0.6 copy-start.11
  41.8 0.9 copy-start.2
  42.7 21.4 %all-to-all-start.1 = ((bf16[32,2,7,1024]{3,1,2,0:T(2,128)(2,1)}), bf16[32,2,7,1024]{3,1,2,0:T(2,128)(2,1)}, u32[]{:S(2)}, u32[]{:S(2)}) async-start(bf16[32,2,7,1024]{3,1,2,0:T(2,128)(2,1)} %copy.71), calls=%async_computation.1 | async-start | bytes 1835008 | tf_op jit(solution)/shard_map/all_to_all | solution.py:82
  64.1 1.7 copy-start.4
  75.2 5.8 %copy-start.23 = (f32[40,8]{0,1:T(8,128)S(1)}, f32[40,8]{0,1:T(8,128)}, u32[]{:S(2)}) copy-start(f32[40,8]{0,1:T(8,128)} %param.21) | copy-start | bytes 3844
  75.2 5.9 %copy-start.16 = (s32[40,8]{1,0:T(8,128)S(1)}, s32[40,8]{1,0:T(8,128)}, u32[]{:S(2)}) copy-start(s32[40,8]{1,0:T(8,128)} %copy-done.15) | copy-start | bytes 3844
  75.2 6.1 %copy-start.12 = (s32[40,64]{0,1:T(8,128)S(1)}, s32[40,64]{0,1:T(8,128)}, u32[]{:S(2)}) copy-start(s32[40,64]{0,1:T(8,128)} %copy-done.11) | copy-start | bytes 30724
  77.1 4.4 %copy-start.24 = (f32[40,8]{0,1:T(8,128)S(1)}, f32[40,8]{0,1:T(8,128)}, u32[]{:S(2)}) copy-start(f32[40,8]{0,1:T(8,128)} %param.20) | copy-start | bytes 3844
  77.1 4.4 %copy-start.14 = (s32[40,8]{1,0:T(8,128)S(1)}, s32[40,8]{1,0:T(8,128)}, u32[]{:S(2)}) copy-start(s32[40,8]{1,0:T(8,128)} %copy-done.13) | copy-start | bytes 3844
  77.1 27.7 %all-to-all-start.3 = ((bf16[32,2,7,1024]{3,1,2,0:T(2,128)(2,1)}), bf16[32,2,7,1024]{3,1,2,0:T(2,128)(2,1)S(1)}, u32[]{:S(2)}, u32[]{:S(2)}) async-start(bf16[32,2,7,1024]{3,1,2,0:T(2,128)(2,1)} %copy.78), calls=%async_computation.3 | async-start | bytes 1835008 | tf_op jit(solution)/shard_map/all_to_all | solution.py:92
  81.8 29.2 %copy-start.10 = (s32[40,64]{0,1:T(8,128)S(1)}, s32[40,64]{0,1:T(8,128)}, u32[]{:S(2)}) copy-start(s32[40,64]{0,1:T(8,128)} %copy-done.9) | copy-start | bytes 30724
  81.8 30.0 %copy-start.20 = (s32[256]{0:T(256)S(1)}, s32[256]{0:T(256)}, u32[]{:S(2)}) copy-start(s32[256]{0:T(256)} %param.28) | copy-start | bytes 3076
  81.8 30.4 %copy-start.28 = (u32[256]{0:T(256)S(1)}, u32[256]{0:T(256)}, u32[]{:S(2)}) copy-start(u32[256]{0:T(256)} %constant.68) | copy-start | bytes 3076
  81.8 31.6 %copy-start.27 = (s32[40]{0:T(128)S(1)}, s32[40]{0:T(128)}, u32[]{:S(2)}) copy-start(s32[40]{0:T(128)} %param.27) | copy-start | bytes 484
  104.8 32.7 %all-to-all-start.2 = ((bf16[32,2,7,1024]{3,1,2,0:T(2,128)(2,1)}), bf16[32,2,7,1024]{3,1,2,0:T(2,128)(2,1)S(1)}, u32[]{:S(2)}, u32[]{:S(2)}) async-start(bf16[32,2,7,1024]{3,1,2,0:T(2,128)(2,1)} %copy.74), calls=%async_computation.2 | async-start | bytes 1835008 | tf_op jit(solution)/shard_map/all_to_all | solution.py:91
  137.5 1.2 copy-start.3
  137.5 1.2 copy-start.6
  137.8 1.6 copy-start.8
  138.7 2.4 copy-start.21
  195.3 13.5 %copy-start.17 = (s32[9728]{0:T(1024)S(1)}, s32[9728]{0:T(1024)}, u32[]{:S(2)}) copy-start(s32[9728]{0:T(1024)} %iota_add_fusion) | copy-start | bytes 116740
  208.8 66.7 %copy-start.26 = (s32[256]{0:T(256)S(1)}, s32[256]{0:T(256)}, u32[]{:S(2)}) copy-start(s32[256]{0:T(256)} %get-tuple-element.67) | copy-start | bytes 3076
  208.8 66.7 %copy-start.29 = (s32[40]{0:T(128)S(1)}, s32[40]{0:T(128)}, u32[]{:S(2)}) copy-start(s32[40]{0:T(128)} %iota_add_fusion.1) | copy-start | bytes 484
  208.8 161.6 %copy-start.25 = (s32[256]{0:T(256)S(1)}, s32[256]{0:T(256)}, u32[]{:S(2)}) copy-start(s32[256]{0:T(256)} %param.29) | copy-start | bytes 3076
  208.8 162.2 %copy-start.1 = (bf16[2,384,1024]{2,1,0:T(8,128)(2,1)S(1)}, bf16[2,384,1024]{2,1,0:T(8,128)(2,1)}, u32[]{:S(2)}) copy-start(bf16[2,384,1024]{2,1,0:T(8,128)(2,1)} %param.24) | copy-start | bytes 4718596
  (3 other events, 1.8 us)
Sparse Core Ops, SparseCore 0:
  10.6 105.0 all-gather.5
